TPU v7x, 256 devices: a whole 4x4x8 slice. The times are simulated.
256 devices in a mesh: lon: 64 (over z, x, y_hi), probe: 4 (over y_lo, core).
Axes of the slice: x: 4, y: 4 (y_hi: 2, y_lo: 2; y = y_hi * 2 + y_lo), z: 8, core: 2. Of those that a mesh axis runs over, the one named last changes fastest.
Arguments:
- increments: float32 [64, 1536, 8, 256], P('probe', 'lon'), may hold values from -6 to 6
- winds: float32 [2, 1536, 8, 256], P(None, 'lon'), may hold values from -0.2 to 0.2
- obs_weight: float32 [1536, 8, 256], P('lon'), may hold values from 0.1 to 10
Outputs:
- basis: float32 [64, 384, 512], P('probe', 'lon')
- upper: float32 [64, 64], replicated
All inputs are finite; a program needn't handle non-finite values.
Results may differ from a plain program's by a relative error of at most 0.00011.
Values sent between devices are 32-bit elements; how exact they have to be, the bound alone decides.
A program may use at most 128 MiB of HBM per device.

v0:
```python
import jax
import jax.numpy as jnp
from jax import lax
from jax.sharding import PartitionSpec as P


def from_behind(block, axis, distance):
    devices = range(lax.axis_size(axis))
    route = [((i - distance) % len(devices), i) for i in devices]
    return lax.ppermute(block, axis, route)


def butterfly_sum(block, axis):
    count = lax.axis_size(axis)
    if count & count - 1:
        return lax.psum(block, axis)
    distance = 1
    while distance < count:
        route = [(i, i ^ distance) for i in range(count)]
        block = block + lax.ppermute(block, axis, route)
        distance *= 2
    return block


def padded(block, sides, width):
    for axis, dim in sides:
        count = lax.axis_size(axis)
        forward = [(i, i + 1) for i in range(count - 1)]
        forward.append((count - 1, 0))
        backward = [(target, source) for source, target in forward]
        low = lax.ppermute(
            lax.slice_in_dim(block, block.shape[dim] - width, None, axis=dim), axis, forward
        )
        high = lax.ppermute(lax.slice_in_dim(block, 0, width, axis=dim), axis, backward)
        block = jnp.concatenate([low, block, high], axis=dim)
    return block


def lat_mask(field):
    rows = lax.broadcasted_iota(jnp.int32, field.shape, field.ndim - 1)
    return jnp.where(rows > 0, field, jnp.zeros_like(field))


def below(field):
    return jnp.concatenate([jnp.zeros_like(field[..., :1]), field[..., :-1]], axis=-1)


def above(field):
    return jnp.concatenate([field[..., 1:], jnp.zeros_like(field[..., :1])], axis=-1)


def forward_core(widened, east, north):
    a_pos = jnp.maximum(east, 0.0)
    b_neg = jnp.minimum(east, 0.0)
    c_pos = jnp.maximum(north[1:-1], 0.0)
    d_neg = jnp.minimum(north[1:-1], 0.0)
    flux_w = a_pos[1:] * widened[:, :-1] + b_neg[1:] * widened[:, 1:]
    inner = widened[:, 1:-1]
    flux_s = c_pos * below(inner) + d_neg * inner
    flux_n = above(flux_s)
    return inner - (flux_w[:, 1:] - flux_w[:, :-1]) - (flux_n - flux_s)


def adjoint_core(widened, east, north):
    a_pos = jnp.maximum(east, 0.0)
    b_neg = jnp.minimum(east, 0.0)[1:-1]
    c_pos = jnp.maximum(north[1:-1], 0.0)
    d_neg = jnp.minimum(north[1:-1], 0.0)
    a_east = a_pos[2:]
    c_north = above(c_pos)
    inner = widened[:, 1:-1]
    west_val = widened[:, :-2]
    east_val = widened[:, 2:]
    return (
        inner * (1.0 - a_east + b_neg - c_north + d_neg)
        - b_neg * west_val
        + a_east * east_val
        - d_neg * below(inner)
        + c_north * above(inner)
    )


def body(increments, winds, obs_weight):
    east_local = winds[0]
    north_local = lat_mask(winds[1])
    next_first = from_behind(east_local[:1], "lon", -1)
    near_east = jnp.concatenate([jnp.zeros_like(next_first), east_local, next_first], axis=0)
    edge_zero = jnp.zeros_like(north_local[:1])
    near_north = jnp.concatenate([edge_zero, north_local, edge_zero], axis=0)

    def widen(field):
        return padded(field, (("lon", 1),), 1)

    state = increments
    for step in range(2):
        state = forward_core(widen(state), near_east, near_north)
    state = obs_weight * state
    for step in range(2):
        state = adjoint_core(widen(state), near_east, near_north)
    sketch = increments + state
    probe_count, lon_count, level_count, lat_count = sketch.shape
    coarse = jnp.mean(
        sketch.reshape(probe_count, lon_count // 4, 4, level_count, lat_count // 4, 4), axis=(2, 5)
    )
    coarse = coarse.reshape(probe_count, -1)
    all_probes = probe_count * lax.axis_size("probe")
    ident = jnp.eye(all_probes, dtype=jnp.float32)
    full_panel = lax.all_gather(coarse, "probe", axis=0, tiled=True)
    local_gram = jnp.dot(
        full_panel,
        full_panel.T,
        precision=lax.Precision.HIGHEST,
        preferred_element_type=jnp.float32,
    )
    gram = butterfly_sum(local_gram, "lon")
    lower = jnp.linalg.cholesky(gram)
    inverse = lax.linalg.triangular_solve(lower, ident, left_side=True, lower=True)
    own_rows = lax.dynamic_slice_in_dim(
        inverse, lax.axis_index("probe") * probe_count, probe_count, 0
    )
    basis = jnp.dot(
        own_rows, full_panel, precision=lax.Precision.HIGHEST, preferred_element_type=jnp.float32
    )
    return (basis.reshape(probe_count, lon_count // 4, -1), lower.T)


def solution(mesh):
    in_specs = (P("probe", "lon", None, None), P(None, "lon", None, None), P("lon", None, None))
    out_specs = (P("probe", "lon", None), P())
    return jax.shard_map(body, mesh=mesh, in_specs=in_specs, out_specs=out_specs, check_vma=False)
```

profile of v0, /device:TPU:8, one launch (start us, length us, event | category | flops | bytes accessed | tf_op | source)
XLA Modules:
  0.0 148.9 jit_solution(1681838737861612050)
XLA Ops:
  0.6 0.7 slice_bitcast_fusion.1
  1.3 9.8 %collective-permute-start = (f32[1,8,256]{2,1,0:T(8,128)S(1)}, f32[1,8,256]{2,1,0:T(8,128)S(1)}, u32[]{:S(2)}, u32[]{:S(2)}) collective-permute-start(f32[1,8,256]{2,1,0:T(8,128)S(1)} %slice_bitcast_fusion.1), channel_id=1, source_target_pairs={{4,0},{8,4},{12,8},{16,12},{20,16},{24,20},{28,24},{32,28},{36,32}... | collective-permute-start | bytes 24584 | tf_op jit(solution)/shard_map/ppermute | solution.py:10
  11.1 1.0 fusion.34
  12.2 7.7 %collective-permute-start.2 = (f32[16,1,8,256]{3,2,1,0:T(8,128)S(1)}, f32[16,1,8,256]{3,2,1,0:T(8,128)S(1)}, u32[]{:S(2)}, u32[]{:S(2)}) collective-permute-start(f32[16,1,8,256]{3,2,1,0:T(8,128)S(1)} %get-tuple-element.22), channel_id=1, source_target_pairs={{4,0},{8,4},{12,8},{16,12},{20,16},{24,20},{28,24},{32,28},{36,32}... | collective-permute-start | bytes 393224 | tf_op jit(solution)/shard_map/ppermute | solution.py:34
  19.9 1.1 maximum_bitcast_fusion
  21.0 0.9 bitcast_select_fusion
  21.9 3.7 %multiply_add_fusion.1 = f32[16,24,8,256]{3,2,1,0:T(8,128)S(1)} fusion(f32[16,24,8,256]{3,2,1,0:T(8,128)} %param.3, f32[16,24,8,255]{3,2,1,0:T(8,128)} %bitcast.37, f32[24,8,256]{2,1,0:T(8,128)S(1)} %get-tuple-element.25, f32[24,8,256]{2,1,0:T(8,128)S(1)} %get-tuple-element.24), kind=kLoop, calls=%fused_computation.31 | loop fusion | flops 2359296 | bytes 9818112 | tf_op jit(solution)/shard_map/add | solution.py:59
  25.7 0.1 slice_maximum_fusion
  25.8 0.9 slice.164
  26.7 0.1 fusion.21
  27.0 0.8 copy-done
  27.8 0.4 fusion
  28.2 1.0 fusion.19
  29.3 7.7 %collective-permute-start.4 = (f32[16,1,8,256]{3,2,1,0:T(8,128)S(1)}, f32[16,1,8,256]{3,2,1,0:T(8,128)S(1)}, u32[]{:S(2)}, u32[]{:S(2)}) collective-permute-start(f32[16,1,8,256]{3,2,1,0:T(8,128)S(1)} %get-tuple-element.20), channel_id=1, source_target_pairs={{4,0},{8,4},{12,8},{16,12},{20,16},{24,20},{28,24},{32,28},{36,32}... | collective-permute-start | bytes 393224 | tf_op jit(solution)/shard_map/ppermute | solution.py:34
  37.1 1.0 multiply_add_fusion
  38.1 2.5 %slice.170 = f32[16,24,8,255]{3,2,1,0:T(8,128)} slice(f32[16,24,8,256]{3,2,1,0:T(8,128)S(1)} %multiply_add_fusion), slice={[0:16], [0:24], [0:8], [1:256]} | slice | bytes 6266880 | tf_op jit(solution)/shard_map/slice | solution.py:49
  40.6 0.4 fusion.1
  41.0 0.5 copy-done.8
  41.5 2.8 %fusion.17 = f32[16,24,8,256]{3,2,1,0:T(8,128)S(1)} fusion(f32[16,24,8,256]{3,2,1,0:T(8,128)S(1)} %fusion.19, f32[16,25,8,256]{3,2,1,0:T(8,128)S(1)} %fusion.1, f32[16,24,8,256]{3,2,1,0:T(8,128)S(1)} %multiply_add_fusion, f32[16,24,8,255]{3,2,1,0:T(8,128)} %slice.170, f32[24,8,256]{2,1,0:T(8,128)S(1)} %copy-done.8), kind=kLoop, calls=%fused_computation.26 | loop fusion | flops 3932160 | bytes 19058688 | tf_op jit(solution)/shard_map/mul | solution.py:97
  44.5 7.7 %collective-permute-start.6 = (f32[16,1,8,256]{3,2,1,0:T(8,128)S(1)}, f32[16,1,8,256]{3,2,1,0:T(8,128)S(1)}, u32[]{:S(2)}, u32[]{:S(2)}) collective-permute-start(f32[16,1,8,256]{3,2,1,0:T(8,128)S(1)} %get-tuple-element.19), channel_id=1, source_target_pairs={{4,0},{8,4},{12,8},{16,12},{20,16},{24,20},{28,24},{32,28},{36,32}... | collective-permute-start | bytes 393224 | tf_op jit(solution)/shard_map/ppermute | solution.py:34
  52.2 1.1 fusion.31
  53.3 1.8 %collective-permute-done.5 = f32[16,1,8,256]{3,2,1,0:T(8,128)S(1)} collective-permute-done((f32[16,1,8,256]{3,2,1,0:T(8,128)S(1)}, f32[16,1,8,256]{3,2,1,0:T(8,128)S(1)}, u32[]{:S(2)}, u32[]{:S(2)}) %collective-permute-start.5) | collective-permute-done | bytes 131104 | tf_op jit(solution)/shard_map/ppermute | solution.py:31
  55.2 2.2 %fusion.12 = f32[16,24,8,256]{3,2,1,0:T(8,128)S(1)} fusion(f32[16,1,8,256]{3,2,1,0:T(8,128)S(1)} %collective-permute-done.6, f32[16,24,8,256]{3,2,1,0:T(8,128)S(1)} %fusion.17, f32[16,1,8,256]{3,2,1,0:T(8,128)S(1)} %collective-permute-done.5, f32[16,24,8,255]{3,2,1,0:T(8,128)S(1)} %get-tuple-element.17, f32[16,24,8,255]{3,2,1,0:T(8,128)S(1)} %get-tuple-element.16, ...), kind=kLoop, calls=%fused_computation.19 | loop fusion | flops 8650752 | bytes 13803520 | tf_op jit(solution)/shard_map/add | solution.py:75
  57.5 7.8 %collective-permute-start.8 = (f32[16,1,8,256]{3,2,1,0:T(8,128)S(1)}, f32[16,1,8,256]{3,2,1,0:T(8,128)S(1)}, u32[]{:S(2)}, u32[]{:S(2)}) collective-permute-start(f32[16,1,8,256]{3,2,1,0:T(8,128)S(1)} %get-tuple-element.15), channel_id=1, source_target_pairs={{4,0},{8,4},{12,8},{16,12},{20,16},{24,20},{28,24},{32,28},{36,32}... | collective-permute-start | bytes 393224 | tf_op jit(solution)/shard_map/ppermute | solution.py:34
  65.3 1.2 fusion.29
  66.5 1.7 %collective-permute-done.7 = f32[16,1,8,256]{3,2,1,0:T(8,128)S(1)} collective-permute-done((f32[16,1,8,256]{3,2,1,0:T(8,128)S(1)}, f32[16,1,8,256]{3,2,1,0:T(8,128)S(1)}, u32[]{:S(2)}, u32[]{:S(2)}) %collective-permute-start.7) | collective-permute-done | bytes 131104 | tf_op jit(solution)/shard_map/ppermute | solution.py:31
  68.2 2.6 %fusion.6 = f32[16,24,8,256]{3,2,1,0:T(8,128)S(1)} fusion(f32[16,24,8,256]{3,2,1,0:T(8,128)S(1)} %copy-done, f32[16,1,8,256]{3,2,1,0:T(8,128)S(1)} %collective-permute-done.8, f32[16,24,8,256]{3,2,1,0:T(8,128)S(1)} %fusion.12, f32[16,1,8,256]{3,2,1,0:T(8,128)S(1)} %collective-permute-done.7, f32[16,24,8,255]{3,2,1,0:T(8,128)S(1)} %get-tuple-element.13, ...), kind=kLoop, calls=%fused_computation.11 | loop fusion | flops 9437184 | bytes 16949248 | tf_op jit(solution)/shard_map/add | solution.py:100
  70.8 12.0 %copy.29 = f32[16,24,8,256]{0,2,3,1:T(8,128)} copy(f32[16,24,8,256]{3,2,1,0:T(8,128)S(1)} %fusion.6) | data formatting | bytes 6291456 | tf_op jit(solution)/shard_map/add | solution.py:100
  82.9 10.1 %reduce_sum.9 = f32[16,6,8,64]{0,2,3,1:T(8,128)S(1)} reduce(f32[16,6,4,8,64,4]{0,3,5,4,2,1:T(8,128)} %bitcast.36, f32[]{:T(128)} %constant.53.clone.1), dimensions={2,5}, to_apply=%region_0.1 | reduce | flops 737280 | bytes 3342340 | tf_op jit(solution)/shard_map/reduce_sum | solution.py:102
  93.0 0.5 copy.30
  93.6 0.2 div.18
  93.7 8.5 %all_gather.3 = f32[64,3072]{1,0:T(8,128)S(1)} all-gather(f32[16,3072]{1,0:T(8,128)S(1)} %div.18), channel_id=1, replica_groups=mesh['lon'=64,'probe'=4] {'probe'}, dimensions={0}, use_global_device_ids=true | all-gather | bytes 983040 | tf_op jit(solution)/shard_map/all_gather | solution.py:108
  102.2 0.8 fusion.35
  103.1 5.4 %collective-permute-done.9 = f32[64,64]{0,1:T(8,128)S(1)} collective-permute-done((f32[64,64]{0,1:T(8,128)S(1)}, f32[64,64]{0,1:T(8,128)S(1)}, u32[]{:S(2)}, u32[]{:S(2)}) %collective-permute-start.9) | collective-permute-done | bytes 16416 | tf_op jit(solution)/shard_map/ppermute | solution.py:20
  108.5 3.9 %collective-permute-done.10 = f32[64,64]{0,1:T(8,128)S(1)} collective-permute-done((f32[64,64]{0,1:T(8,128)S(1)}, f32[64,64]{0,1:T(8,128)S(1)}, u32[]{:S(2)}, u32[]{:S(2)}) %collective-permute-start.10) | collective-permute-done | bytes 16416 | tf_op jit(solution)/shard_map/ppermute | solution.py:20
  112.4 5.4 %collective-permute-done.11 = f32[64,64]{0,1:T(8,128)S(1)} collective-permute-done((f32[64,64]{0,1:T(8,128)S(1)}, f32[64,64]{0,1:T(8,128)S(1)}, u32[]{:S(2)}, u32[]{:S(2)}) %collective-permute-start.11) | collective-permute-done | bytes 16416 | tf_op jit(solution)/shard_map/ppermute | solution.py:20
  117.8 4.2 %collective-permute-done.12 = f32[64,64]{0,1:T(8,128)S(1)} collective-permute-done((f32[64,64]{0,1:T(8,128)S(1)}, f32[64,64]{0,1:T(8,128)S(1)}, u32[]{:S(2)}, u32[]{:S(2)}) %collective-permute-start.12) | collective-permute-done | bytes 16416 | tf_op jit(solution)/shard_map/ppermute | solution.py:20
  122.0 4.8 %collective-permute-done.13 = f32[64,64]{0,1:T(8,128)S(1)} collective-permute-done((f32[64,64]{0,1:T(8,128)S(1)}, f32[64,64]{0,1:T(8,128)S(1)}, u32[]{:S(2)}, u32[]{:S(2)}) %collective-permute-start.13) | collective-permute-done | bytes 16416 | tf_op jit(solution)/shard_map/ppermute | solution.py:20
  126.8 1.5 collective-permute-start.14
  128.3 6.3 %collective-permute-done.14 = f32[64,64]{0,1:T(8,128)S(1)} collective-permute-done((f32[64,64]{0,1:T(8,128)S(1)}, f32[64,64]{0,1:T(8,128)S(1)}, u32[]{:S(2)}, u32[]{:S(2)}) %collective-permute-start.14) | collective-permute-done | bytes 16416 | tf_op jit(solution)/shard_map/ppermute | solution.py:20
  134.7 5.8 %cholesky.17 = f32[64,64]{1,0:T(8,128)S(1)} custom-call(f32[64,64]{1,0:T(8,128)S(1)} %fusion.24), custom_call_target="Cholesky" | custom-call | tf_op jit(solution)/shard_map/jit(cholesky)/cholesky | solution.py:116
  140.6 0.6 compare_reduce_fusion
  141.3 0.7 fusion.25
  141.9 4.9 %custom-call.6 = f32[1,64,64]{1,2,0:T(8,128)S(1)} custom-call(f32[1,64,64]{2,1,0:T(8,128)S(1)} %get-tuple-element.34), custom_call_target="InvertDiagBlocksLowerTriangular" | custom-call | tf_op jit(solution)/shard_map/triangular_solve | solution.py:117
  146.8 0.2 fusion.22
  147.1 0.5 fusion.26
  147.6 0.7 copy.39
  148.2 0.7 copy.35
  (50 shorter events, 0.8 us)
Async XLA Ops:
  1.3 25.4 %collective-permute-start = (f32[1,8,256]{2,1,0:T(8,128)S(1)}, f32[1,8,256]{2,1,0:T(8,128)S(1)}, u32[]{:S(2)}, u32[]{:S(2)}) collective-permute-start(f32[1,8,256]{2,1,0:T(8,128)S(1)} %slice_bitcast_fusion.1), channel_id=1, source_target_pairs={{4,0},{8,4},{12,8},{16,12},{20,16},{24,20},{28,24},{32,28},{36,32}... | collective-permute-start | bytes 24584 | tf_op jit(solution)/shard_map/ppermute | solution.py:10
  12.1 14.9 %collective-permute-start.1 = (f32[16,1,8,256]{3,2,1,0:T(8,128)S(1)}, f32[16,1,8,256]{3,2,1,0:T(8,128)S(1)}, u32[]{:S(2)}, u32[]{:S(2)}) collective-permute-start(f32[16,1,8,256]{3,2,1,0:T(8,128)S(1)} %get-tuple-element.23), channel_id=1, source_target_pairs={{0,4},{4,8},{8,12},{12,16},{16,20},{20,24},{24,28},{28,32},{32,36}... | collective-permute-start | bytes 393224 | tf_op jit(solution)/shard_map/ppermute | solution.py:31
  12.2 14.8 %collective-permute-start.2 = (f32[16,1,8,256]{3,2,1,0:T(8,128)S(1)}, f32[16,1,8,256]{3,2,1,0:T(8,128)S(1)}, u32[]{:S(2)}, u32[]{:S(2)}) collective-permute-start(f32[16,1,8,256]{3,2,1,0:T(8,128)S(1)} %get-tuple-element.22), channel_id=1, source_target_pairs={{4,0},{8,4},{12,8},{16,12},{20,16},{24,20},{28,24},{32,28},{36,32}... | collective-permute-start | bytes 393224 | tf_op jit(solution)/shard_map/ppermute | solution.py:34
  25.8 1.1 copy-start.7
  25.8 2.0 %copy-start = (f32[16,24,8,256]{3,2,1,0:T(8,128)S(1)}, f32[16,24,8,256]{3,2,1,0:T(8,128)}, u32[]{:S(2)}) copy-start(f32[16,24,8,256]{3,2,1,0:T(8,128)} %param.3) | copy-start | bytes 9437188
  27.0 28.2 %copy-start.1 = (f32[24,8,256]{2,1,0:T(8,128)}, f32[24,8,256]{2,1,0:T(8,128)S(1)}, u32[]{:S(2)}) copy-start(f32[24,8,256]{2,1,0:T(8,128)S(1)} %get-tuple-element.28) | copy-start | bytes 589828
  27.0 28.2 %copy-start.3 = (f32[24,8,256]{2,1,0:T(8,128)}, f32[24,8,256]{2,1,0:T(8,128)S(1)}, u32[]{:S(2)}) copy-start(f32[24,8,256]{2,1,0:T(8,128)S(1)} %get-tuple-element.29) | copy-start | bytes 589828
  27.0 28.2 %copy-start.5 = (f32[24,8,256]{2,1,0:T(8,128)}, f32[24,8,256]{2,1,0:T(8,128)S(1)}, u32[]{:S(2)}) copy-start(f32[24,8,256]{2,1,0:T(8,128)S(1)} %get-tuple-element.32) | copy-start | bytes 589828
  29.3 11.3 %collective-permute-start.3 = (f32[16,1,8,256]{3,2,1,0:T(8,128)S(1)}, f32[16,1,8,256]{3,2,1,0:T(8,128)S(1)}, u32[]{:S(2)}, u32[]{:S(2)}) collective-permute-start(f32[16,1,8,256]{3,2,1,0:T(8,128)S(1)} %get-tuple-element.21), channel_id=1, source_target_pairs={{0,4},{4,8},{8,12},{12,16},{16,20},{20,24},{24,28},{28,32},{32,36}... | collective-permute-start | bytes 393224 | tf_op jit(solution)/shard_map/ppermute | solution.py:31
  29.3 11.2 %collective-permute-start.4 = (f32[16,1,8,256]{3,2,1,0:T(8,128)S(1)}, f32[16,1,8,256]{3,2,1,0:T(8,128)S(1)}, u32[]{:S(2)}, u32[]{:S(2)}) collective-permute-start(f32[16,1,8,256]{3,2,1,0:T(8,128)S(1)} %get-tuple-element.20), channel_id=1, source_target_pairs={{4,0},{8,4},{12,8},{16,12},{20,16},{24,20},{28,24},{32,28},{36,32}... | collective-permute-start | bytes 393224 | tf_op jit(solution)/shard_map/ppermute | solution.py:34
  40.6 0.9 copy-start.8
  44.4 10.8 %collective-permute-start.5 = (f32[16,1,8,256]{3,2,1,0:T(8,128)S(1)}, f32[16,1,8,256]{3,2,1,0:T(8,128)S(1)}, u32[]{:S(2)}, u32[]{:S(2)}) collective-permute-start(f32[16,1,8,256]{3,2,1,0:T(8,128)S(1)} %get-tuple-element.18), channel_id=1, source_target_pairs={{0,4},{4,8},{8,12},{12,16},{16,20},{20,24},{24,28},{28,32},{32,36}... | collective-permute-start | bytes 393224 | tf_op jit(solution)/shard_map/ppermute | solution.py:31
  44.5 10.7 %collective-permute-start.6 = (f32[16,1,8,256]{3,2,1,0:T(8,128)S(1)}, f32[16,1,8,256]{3,2,1,0:T(8,128)S(1)}, u32[]{:S(2)}, u32[]{:S(2)}) collective-permute-start(f32[16,1,8,256]{3,2,1,0:T(8,128)S(1)} %get-tuple-element.19), channel_id=1, source_target_pairs={{4,0},{8,4},{12,8},{16,12},{20,16},{24,20},{28,24},{32,28},{36,32}... | collective-permute-start | bytes 393224 | tf_op jit(solution)/shard_map/ppermute | solution.py:34
  57.4 10.8 %collective-permute-start.7 = (f32[16,1,8,256]{3,2,1,0:T(8,128)S(1)}, f32[16,1,8,256]{3,2,1,0:T(8,128)S(1)}, u32[]{:S(2)}, u32[]{:S(2)}) collective-permute-start(f32[16,1,8,256]{3,2,1,0:T(8,128)S(1)} %get-tuple-element.14), channel_id=1, source_target_pairs={{0,4},{4,8},{8,12},{12,16},{16,20},{20,24},{24,28},{28,32},{32,36}... | collective-permute-start | bytes 393224 | tf_op jit(solution)/shard_map/ppermute | solution.py:31
  57.5 10.7 %copy-start.2 = (f32[24,8,256]{2,1,0:T(8,128)S(1)}, f32[24,8,256]{2,1,0:T(8,128)}, u32[]{:S(2)}) copy-start(f32[24,8,256]{2,1,0:T(8,128)} %copy-done.1) | copy-start | bytes 589828
  57.5 10.7 %copy-start.4 = (f32[24,8,256]{2,1,0:T(8,128)S(1)}, f32[24,8,256]{2,1,0:T(8,128)}, u32[]{:S(2)}) copy-start(f32[24,8,256]{2,1,0:T(8,128)} %copy-done.3) | copy-start | bytes 589828
  57.5 10.7 %copy-start.6 = (f32[24,8,256]{2,1,0:T(8,128)S(1)}, f32[24,8,256]{2,1,0:T(8,128)}, u32[]{:S(2)}) copy-start(f32[24,8,256]{2,1,0:T(8,128)} %copy-done.5) | copy-start | bytes 589828
  57.5 10.6 %collective-permute-start.8 = (f32[16,1,8,256]{3,2,1,0:T(8,128)S(1)}, f32[16,1,8,256]{3,2,1,0:T(8,128)S(1)}, u32[]{:S(2)}, u32[]{:S(2)}) collective-permute-start(f32[16,1,8,256]{3,2,1,0:T(8,128)S(1)} %get-tuple-element.15), channel_id=1, source_target_pairs={{4,0},{8,4},{12,8},{16,12},{20,16},{24,20},{28,24},{32,28},{36,32}... | collective-permute-start | bytes 393224 | tf_op jit(solution)/shard_map/ppermute | solution.py:34
  103.0 5.5 %collective-permute-start.9 = (f32[64,64]{0,1:T(8,128)S(1)}, f32[64,64]{0,1:T(8,128)S(1)}, u32[]{:S(2)}, u32[]{:S(2)}) collective-permute-start(f32[64,64]{0,1:T(8,128)S(1)} %fusion.35), channel_id=1, source_target_pairs={{0,4},{4,0},{8,12},{12,8},{16,20},{20,16},{24,28},{28,24},{32,36},... | collective-permute-start | bytes 49160 | tf_op jit(solution)/shard_map/ppermute | solution.py:20
  108.5 3.9 %collective-permute-start.10 = (f32[64,64]{0,1:T(8,128)S(1)}, f32[64,64]{0,1:T(8,128)S(1)}, u32[]{:S(2)}, u32[]{:S(2)}) collective-permute-start(f32[64,64]{0,1:T(8,128)S(1)} %add.96), channel_id=1, source_target_pairs={{0,8},{4,12},{8,0},{12,4},{16,24},{20,28},{24,16},{28,20},{32,40},... | collective-permute-start | bytes 49160 | tf_op jit(solution)/shard_map/ppermute | solution.py:20
  112.4 5.4 %collective-permute-start.11 = (f32[64,64]{0,1:T(8,128)S(1)}, f32[64,64]{0,1:T(8,128)S(1)}, u32[]{:S(2)}, u32[]{:S(2)}) collective-permute-start(f32[64,64]{0,1:T(8,128)S(1)} %add.97), channel_id=1, source_target_pairs={{0,16},{4,20},{8,24},{12,28},{16,0},{20,4},{24,8},{28,12},{32,48},... | collective-permute-start | bytes 49160 | tf_op jit(solution)/shard_map/ppermute | solution.py:20
  117.8 4.2 %collective-permute-start.12 = (f32[64,64]{0,1:T(8,128)S(1)}, f32[64,64]{0,1:T(8,128)S(1)}, u32[]{:S(2)}, u32[]{:S(2)}) collective-permute-start(f32[64,64]{0,1:T(8,128)S(1)} %add.98), channel_id=1, source_target_pairs={{0,32},{4,36},{8,40},{12,44},{16,48},{20,52},{24,56},{28,60},{32,0... | collective-permute-start | bytes 49160 | tf_op jit(solution)/shard_map/ppermute | solution.py:20
  122.0 4.8 %collective-permute-start.13 = (f32[64,64]{0,1:T(8,128)S(1)}, f32[64,64]{0,1:T(8,128)S(1)}, u32[]{:S(2)}, u32[]{:S(2)}) collective-permute-start(f32[64,64]{0,1:T(8,128)S(1)} %add.99), channel_id=1, source_target_pairs={{0,64},{4,68},{8,72},{12,76},{16,80},{20,84},{24,88},{28,92},{32,9... | collective-permute-start | bytes 49160 | tf_op jit(solution)/shard_map/ppermute | solution.py:20
  126.8 7.8 %collective-permute-start.14 = (f32[64,64]{0,1:T(8,128)S(1)}, f32[64,64]{0,1:T(8,128)S(1)}, u32[]{:S(2)}, u32[]{:S(2)}) collective-permute-start(f32[64,64]{0,1:T(8,128)S(1)} %add.100), channel_id=1, source_target_pairs={{0,128},{4,132},{8,136},{12,140},{16,144},{20,148},{24,152},{28,15... | collective-permute-start | bytes 49160 | tf_op jit(solution)/shard_map/ppermute | solution.py:20
where the time goes:
time: 149 us
  starting transfers between devices  42.7 us (29%)
  other arithmetic  38.7 us (26%)
  waiting for transfers between devices  33.5 us (22%)
  local copies, waits for them, and re-layouts  23 us (15%)
  blocking collectives  8.45 us (6%)
    ppermute x4, starting transfers between devices, padded(): lax.ppermute(lax.slice_in_dim(block, 0, width, axis=dim), axis, backward)  31 us
    ppermute x6, waiting for transfers between devices, butterfly_sum(): block = block + lax.ppermute(block, axis, route)  30 us
    add x1, local copies, waits for them, and re-layouts, body(): sketch = increments + state  12 us
    reduce_sum x1, other arithmetic, body(): jnp.mean(sketch.reshape(probe_count, lon_count // 4, 4, level_count, lat_...  10.1 us
    ppermute x1, starting transfers between devices, from_behind(): return lax.ppermute(block, axis, route)  9.78 us
    all_gather x1, blocking collectives, body(): full_panel = lax.all_gather(coarse, 'probe', axis=0, tiled=True)  8.45 us
    another operation x3, other arithmetic, body(): lower = jnp.linalg.cholesky(gram)  6.52 us
    another operation x1, other arithmetic, body(): lax.linalg.triangular_solve(lower, ident, left_side=True, lower=True)  4.9 us
  transfers between devices with their start and end apart: 15, of which 8 were waited for; matrix products, arithmetic and copies ran while one was open for 9% of the time, Pallas kernels for 0%

commit v1 on v0

--- a/solution.py
+++ b/solution.py
@@ -2,6 +2,7 @@
 import jax.numpy as jnp
 from jax import lax
 from jax.sharding import PartitionSpec as P
+from jax.lax import all_to_all, axis_size
 
 
 def from_behind(block, axis, distance):
@@ -105,7 +106,9 @@
     coarse = coarse.reshape(probe_count, -1)
     all_probes = probe_count * lax.axis_size("probe")
     ident = jnp.eye(all_probes, dtype=jnp.float32)
-    full_panel = lax.all_gather(coarse, "probe", axis=0, tiled=True)
+    full_panel = jnp.concatenate(
+        all_to_all(jnp.stack([coarse for _ in range(axis_size("probe"))], 0), "probe", 0, 0), 0
+    )
     local_gram = jnp.dot(
         full_panel,
         full_panel.T,

time: 149 us -> 155 us (1.040)
  blocking collectives: 8.45 us -> 13.7 us
    all_to_all x0 -> x1, blocking collectives: none -> 13.7 us  [body(): all_to_all(jnp.stack([coarse for _ in range(axis_size('probe'))], 0), 'pr...]
    all_gather x1 -> x0, blocking collectives: 8.45 us -> none  [body(): full_panel = lax.all_gather(coarse, 'probe', axis=0, tiled=True)]
where the time goes in v1:
time: 155 us; the launch traced here: 154 us
  starting transfers between devices  43 us (28%)
  other arithmetic  38.7 us (25%)
  waiting for transfers between devices  33.3 us (21%)
  local copies, waits for them, and re-layouts  22.3 us (14%)
  blocking collectives  13.7 us (9%)
  matrix products  2.17 us (1%)
    ppermute x4, starting transfers between devices, padded(): lax.ppermute(lax.slice_in_dim(block, 0, width, axis=dim), axis, backward)  31 us
    ppermute x6, waiting for transfers between devices, butterfly_sum(): block = block + lax.ppermute(block, axis, route)  29.8 us
    all_to_all x1, blocking collectives, body(): all_to_all(jnp.stack([coarse for _ in range(axis_size('probe'))], 0), 'pr...  13.7 us
    add x1, local copies, waits for them, and re-layouts, body(): sketch = increments + state  12 us
    reduce_sum x1, other arithmetic, body(): jnp.mean(sketch.reshape(probe_count, lon_count // 4, 4, level_count, lat_...  10.1 us
    ppermute x1, starting transfers between devices, from_behind(): return lax.ppermute(block, axis, route)  9.78 us
    another operation x3, other arithmetic, body(): lower = jnp.linalg.cholesky(gram)  6.52 us
    another operation x1, other arithmetic, body(): lax.linalg.triangular_solve(lower, ident, left_side=True, lower=True)  4.9 us
  transfers between devices with their start and end apart: 15, of which 8 were waited for; matrix products, arithmetic and copies ran while one was open for 9% of the time, Pallas kernels for 0%

profile of v1, /device:TPU:8, one launch (start us, length us, event | category | flops | bytes accessed | tf_op | source)
XLA Modules:
  0.0 154.4 jit_solution(18442409916778070136)
XLA Ops:
  0.6 0.7 slice_bitcast_fusion.1
  1.3 9.8 %collective-permute-start = (f32[1,8,256]{2,1,0:T(8,128)S(1)}, f32[1,8,256]{2,1,0:T(8,128)S(1)}, u32[]{:S(2)}, u32[]{:S(2)}) collective-permute-start(f32[1,8,256]{2,1,0:T(8,128)S(1)} %slice_bitcast_fusion.1), channel_id=1, source_target_pairs={{4,0},{8,4},{12,8},{16,12},{20,16},{24,20},{28,24},{32,28},{36,32}... | collective-permute-start | bytes 24584 | tf_op jit(solution)/shard_map/ppermute | solution.py:11
  11.1 1.0 fusion.37
  12.2 7.7 %collective-permute-start.2 = (f32[16,1,8,256]{3,2,1,0:T(8,128)S(1)}, f32[16,1,8,256]{3,2,1,0:T(8,128)S(1)}, u32[]{:S(2)}, u32[]{:S(2)}) collective-permute-start(f32[16,1,8,256]{3,2,1,0:T(8,128)S(1)} %get-tuple-element.22), channel_id=1, source_target_pairs={{4,0},{8,4},{12,8},{16,12},{20,16},{24,20},{28,24},{32,28},{36,32}... | collective-permute-start | bytes 393224 | tf_op jit(solution)/shard_map/ppermute | solution.py:35
  19.9 1.1 maximum_bitcast_fusion
  21.0 0.9 bitcast_select_fusion
  21.9 3.7 %multiply_add_fusion.1 = f32[16,24,8,256]{3,2,1,0:T(8,128)S(1)} fusion(f32[16,24,8,256]{3,2,1,0:T(8,128)} %param.3, f32[16,24,8,255]{3,2,1,0:T(8,128)} %bitcast.42, f32[24,8,256]{2,1,0:T(8,128)S(1)} %get-tuple-element.25, f32[24,8,256]{2,1,0:T(8,128)S(1)} %get-tuple-element.24), kind=kLoop, calls=%fused_computation.31 | loop fusion | flops 2359296 | bytes 9818112 | tf_op jit(solution)/shard_map/add | solution.py:60
  25.7 0.1 slice_maximum_fusion
  25.8 0.9 slice.164
  26.7 0.1 fusion.24
  27.0 0.8 copy-done
  27.8 0.4 fusion
  28.2 1.0 fusion.19
  29.3 7.7 %collective-permute-start.4 = (f32[16,1,8,256]{3,2,1,0:T(8,128)S(1)}, f32[16,1,8,256]{3,2,1,0:T(8,128)S(1)}, u32[]{:S(2)}, u32[]{:S(2)}) collective-permute-start(f32[16,1,8,256]{3,2,1,0:T(8,128)S(1)} %get-tuple-element.20), channel_id=1, source_target_pairs={{4,0},{8,4},{12,8},{16,12},{20,16},{24,20},{28,24},{32,28},{36,32}... | collective-permute-start | bytes 393224 | tf_op jit(solution)/shard_map/ppermute | solution.py:35
  37.1 1.0 multiply_add_fusion
  38.1 2.5 %slice.170 = f32[16,24,8,255]{3,2,1,0:T(8,128)} slice(f32[16,24,8,256]{3,2,1,0:T(8,128)S(1)} %multiply_add_fusion), slice={[0:16], [0:24], [0:8], [1:256]} | slice | bytes 6266880 | tf_op jit(solution)/shard_map/slice | solution.py:50
  40.6 0.4 fusion.1
  41.0 0.5 copy-done.8
  41.5 2.8 %fusion.17 = f32[16,24,8,256]{3,2,1,0:T(8,128)S(1)} fusion(f32[16,24,8,256]{3,2,1,0:T(8,128)S(1)} %fusion.19, f32[16,25,8,256]{3,2,1,0:T(8,128)S(1)} %fusion.1, f32[16,24,8,256]{3,2,1,0:T(8,128)S(1)} %multiply_add_fusion, f32[16,24,8,255]{3,2,1,0:T(8,128)} %slice.170, f32[24,8,256]{2,1,0:T(8,128)S(1)} %copy-done.8), kind=kLoop, calls=%fused_computation.26 | loop fusion | flops 3932160 | bytes 19058688 | tf_op jit(solution)/shard_map/mul | solution.py:98
  44.5 7.7 %collective-permute-start.6 = (f32[16,1,8,256]{3,2,1,0:T(8,128)S(1)}, f32[16,1,8,256]{3,2,1,0:T(8,128)S(1)}, u32[]{:S(2)}, u32[]{:S(2)}) collective-permute-start(f32[16,1,8,256]{3,2,1,0:T(8,128)S(1)} %get-tuple-element.19), channel_id=1, source_target_pairs={{4,0},{8,4},{12,8},{16,12},{20,16},{24,20},{28,24},{32,28},{36,32}... | collective-permute-start | bytes 393224 | tf_op jit(solution)/shard_map/ppermute | solution.py:35
  52.2 1.1 fusion.34
  53.3 1.8 %collective-permute-done.5 = f32[16,1,8,256]{3,2,1,0:T(8,128)S(1)} collective-permute-done((f32[16,1,8,256]{3,2,1,0:T(8,128)S(1)}, f32[16,1,8,256]{3,2,1,0:T(8,128)S(1)}, u32[]{:S(2)}, u32[]{:S(2)}) %collective-permute-start.5) | collective-permute-done | bytes 131104 | tf_op jit(solution)/shard_map/ppermute | solution.py:32
  55.2 2.2 %fusion.12 = f32[16,24,8,256]{3,2,1,0:T(8,128)S(1)} fusion(f32[16,1,8,256]{3,2,1,0:T(8,128)S(1)} %collective-permute-done.6, f32[16,24,8,256]{3,2,1,0:T(8,128)S(1)} %fusion.17, f32[16,1,8,256]{3,2,1,0:T(8,128)S(1)} %collective-permute-done.5, f32[16,24,8,255]{3,2,1,0:T(8,128)S(1)} %get-tuple-element.17, f32[16,24,8,255]{3,2,1,0:T(8,128)S(1)} %get-tuple-element.16, ...), kind=kLoop, calls=%fused_computation.19 | loop fusion | flops 8650752 | bytes 13803520 | tf_op jit(solution)/shard_map/add | solution.py:76
  57.5 7.8 %collective-permute-start.8 = (f32[16,1,8,256]{3,2,1,0:T(8,128)S(1)}, f32[16,1,8,256]{3,2,1,0:T(8,128)S(1)}, u32[]{:S(2)}, u32[]{:S(2)}) collective-permute-start(f32[16,1,8,256]{3,2,1,0:T(8,128)S(1)} %get-tuple-element.15), channel_id=1, source_target_pairs={{4,0},{8,4},{12,8},{16,12},{20,16},{24,20},{28,24},{32,28},{36,32}... | collective-permute-start | bytes 393224 | tf_op jit(solution)/shard_map/ppermute | solution.py:35
  65.3 1.2 fusion.32
  66.5 1.7 %collective-permute-done.7 = f32[16,1,8,256]{3,2,1,0:T(8,128)S(1)} collective-permute-done((f32[16,1,8,256]{3,2,1,0:T(8,128)S(1)}, f32[16,1,8,256]{3,2,1,0:T(8,128)S(1)}, u32[]{:S(2)}, u32[]{:S(2)}) %collective-permute-start.7) | collective-permute-done | bytes 131104 | tf_op jit(solution)/shard_map/ppermute | solution.py:32
  68.2 2.6 %fusion.6 = f32[16,24,8,256]{3,2,1,0:T(8,128)S(1)} fusion(f32[16,24,8,256]{3,2,1,0:T(8,128)S(1)} %copy-done, f32[16,1,8,256]{3,2,1,0:T(8,128)S(1)} %collective-permute-done.8, f32[16,24,8,256]{3,2,1,0:T(8,128)S(1)} %fusion.12, f32[16,1,8,256]{3,2,1,0:T(8,128)S(1)} %collective-permute-done.7, f32[16,24,8,255]{3,2,1,0:T(8,128)S(1)} %get-tuple-element.13, ...), kind=kLoop, calls=%fused_computation.11 | loop fusion | flops 9437184 | bytes 16949248 | tf_op jit(solution)/shard_map/add | solution.py:101
  70.8 12.0 %copy.28 = f32[16,24,8,256]{0,2,3,1:T(8,128)} copy(f32[16,24,8,256]{3,2,1,0:T(8,128)S(1)} %fusion.6) | data formatting | bytes 6291456 | tf_op jit(solution)/shard_map/add | solution.py:101
  82.9 10.1 %reduce_sum.9 = f32[16,6,8,64]{0,2,3,1:T(8,128)S(1)} reduce(f32[16,6,4,8,64,4]{0,3,5,4,2,1:T(8,128)} %bitcast.41, f32[]{:T(128)} %constant.53.clone.1), dimensions={2,5}, to_apply=%region_0.1 | reduce | flops 737280 | bytes 3342340 | tf_op jit(solution)/shard_map/reduce_sum | solution.py:103
  93.0 0.5 copy.29
  93.6 0.2 div.18
  93.8 13.7 %all_to_all.5 = f32[4,16,3072]{2,1,0:T(8,128)S(1)} all-to-all(f32[4,16,3072]{2,1,0:T(8,128)S(1)} %stack.3), channel_id=1, replica_groups=mesh['lon'=64,'probe'=4] {'probe'}, dimensions={0} | all-to-all | bytes 1572864 | tf_op jit(solution)/shard_map/all_to_all | solution.py:110
  107.5 0.8 fusion.38
  108.3 0.1 collective-permute-start.9
  108.4 5.4 %collective-permute-done.9 = f32[64,64]{0,1:T(8,128)S(1)} collective-permute-done((f32[64,64]{0,1:T(8,128)S(1)}, f32[64,64]{0,1:T(8,128)S(1)}, u32[]{:S(2)}, u32[]{:S(2)}) %collective-permute-start.9) | collective-permute-done | bytes 16416 | tf_op jit(solution)/shard_map/ppermute | solution.py:21
  113.8 3.9 %collective-permute-done.10 = f32[64,64]{0,1:T(8,128)S(1)} collective-permute-done((f32[64,64]{0,1:T(8,128)S(1)}, f32[64,64]{0,1:T(8,128)S(1)}, u32[]{:S(2)}, u32[]{:S(2)}) %collective-permute-start.10) | collective-permute-done | bytes 16416 | tf_op jit(solution)/shard_map/ppermute | solution.py:21
  117.8 5.4 %collective-permute-done.11 = f32[64,64]{0,1:T(8,128)S(1)} collective-permute-done((f32[64,64]{0,1:T(8,128)S(1)}, f32[64,64]{0,1:T(8,128)S(1)}, u32[]{:S(2)}, u32[]{:S(2)}) %collective-permute-start.11) | collective-permute-done | bytes 16416 | tf_op jit(solution)/shard_map/ppermute | solution.py:21
  123.2 3.9 %collective-permute-done.12 = f32[64,64]{0,1:T(8,128)S(1)} collective-permute-done((f32[64,64]{0,1:T(8,128)S(1)}, f32[64,64]{0,1:T(8,128)S(1)}, u32[]{:S(2)}, u32[]{:S(2)}) %collective-permute-start.12) | collective-permute-done | bytes 16416 | tf_op jit(solution)/shard_map/ppermute | solution.py:21
  127.1 5.2 %collective-permute-done.13 = f32[64,64]{0,1:T(8,128)S(1)} collective-permute-done((f32[64,64]{0,1:T(8,128)S(1)}, f32[64,64]{0,1:T(8,128)S(1)}, u32[]{:S(2)}, u32[]{:S(2)}) %collective-permute-start.13) | collective-permute-done | bytes 16416 | tf_op jit(solution)/shard_map/ppermute | solution.py:21
  132.3 1.8 %collective-permute-start.14 = (f32[64,64]{0,1:T(8,128)S(1)}, f32[64,64]{0,1:T(8,128)S(1)}, u32[]{:S(2)}, u32[]{:S(2)}) collective-permute-start(f32[64,64]{0,1:T(8,128)S(1)} %add.100), channel_id=1, source_target_pairs={{0,128},{4,132},{8,136},{12,140},{16,144},{20,148},{24,152},{28,15... | collective-permute-start | bytes 49160 | tf_op jit(solution)/shard_map/ppermute | solution.py:21
  134.1 6.0 %collective-permute-done.14 = f32[64,64]{0,1:T(8,128)S(1)} collective-permute-done((f32[64,64]{0,1:T(8,128)S(1)}, f32[64,64]{0,1:T(8,128)S(1)}, u32[]{:S(2)}, u32[]{:S(2)}) %collective-permute-start.14) | collective-permute-done | bytes 16416 | tf_op jit(solution)/shard_map/ppermute | solution.py:21
  140.2 5.8 %cholesky.17 = f32[64,64]{1,0:T(8,128)S(1)} custom-call(f32[64,64]{1,0:T(8,128)S(1)} %fusion.27), custom_call_target="Cholesky" | custom-call | tf_op jit(solution)/shard_map/jit(cholesky)/cholesky | solution.py:119
  146.1 0.6 compare_reduce_fusion
  146.7 0.7 fusion.28
  147.4 4.9 %custom-call.6 = f32[1,64,64]{1,2,0:T(8,128)S(1)} custom-call(f32[1,64,64]{2,1,0:T(8,128)S(1)} %get-tuple-element.34), custom_call_target="InvertDiagBlocksLowerTriangular" | custom-call | tf_op jit(solution)/shard_map/triangular_solve | solution.py:120
  152.3 0.2 fusion.25
  152.5 0.7 copy.34
  153.2 1.2 fusion.20
  (50 shorter events, 0.8 us)
Async XLA Ops:
  1.3 25.4 %collective-permute-start = (f32[1,8,256]{2,1,0:T(8,128)S(1)}, f32[1,8,256]{2,1,0:T(8,128)S(1)}, u32[]{:S(2)}, u32[]{:S(2)}) collective-permute-start(f32[1,8,256]{2,1,0:T(8,128)S(1)} %slice_bitcast_fusion.1), channel_id=1, source_target_pairs={{4,0},{8,4},{12,8},{16,12},{20,16},{24,20},{28,24},{32,28},{36,32}... | collective-permute-start | bytes 24584 | tf_op jit(solution)/shard_map/ppermute | solution.py:11
  12.1 14.9 %collective-permute-start.1 = (f32[16,1,8,256]{3,2,1,0:T(8,128)S(1)}, f32[16,1,8,256]{3,2,1,0:T(8,128)S(1)}, u32[]{:S(2)}, u32[]{:S(2)}) collective-permute-start(f32[16,1,8,256]{3,2,1,0:T(8,128)S(1)} %get-tuple-element.23), channel_id=1, source_target_pairs={{0,4},{4,8},{8,12},{12,16},{16,20},{20,24},{24,28},{28,32},{32,36}... | collective-permute-start | bytes 393224 | tf_op jit(solution)/shard_map/ppermute | solution.py:32
  12.2 14.8 %collective-permute-start.2 = (f32[16,1,8,256]{3,2,1,0:T(8,128)S(1)}, f32[16,1,8,256]{3,2,1,0:T(8,128)S(1)}, u32[]{:S(2)}, u32[]{:S(2)}) collective-permute-start(f32[16,1,8,256]{3,2,1,0:T(8,128)S(1)} %get-tuple-element.22), channel_id=1, source_target_pairs={{4,0},{8,4},{12,8},{16,12},{20,16},{24,20},{28,24},{32,28},{36,32}... | collective-permute-start | bytes 393224 | tf_op jit(solution)/shard_map/ppermute | solution.py:35
  25.8 1.1 copy-start.7
  25.8 2.0 %copy-start = (f32[16,24,8,256]{3,2,1,0:T(8,128)S(1)}, f32[16,24,8,256]{3,2,1,0:T(8,128)}, u32[]{:S(2)}) copy-start(f32[16,24,8,256]{3,2,1,0:T(8,128)} %param.3) | copy-start | bytes 9437188
  27.0 28.2 %copy-start.1 = (f32[24,8,256]{2,1,0:T(8,128)}, f32[24,8,256]{2,1,0:T(8,128)S(1)}, u32[]{:S(2)}) copy-start(f32[24,8,256]{2,1,0:T(8,128)S(1)} %get-tuple-element.28) | copy-start | bytes 589828
  27.0 28.2 %copy-start.3 = (f32[24,8,256]{2,1,0:T(8,128)}, f32[24,8,256]{2,1,0:T(8,128)S(1)}, u32[]{:S(2)}) copy-start(f32[24,8,256]{2,1,0:T(8,128)S(1)} %get-tuple-element.29) | copy-start | bytes 589828
  27.0 28.2 %copy-start.5 = (f32[24,8,256]{2,1,0:T(8,128)}, f32[24,8,256]{2,1,0:T(8,128)S(1)}, u32[]{:S(2)}) copy-start(f32[24,8,256]{2,1,0:T(8,128)S(1)} %get-tuple-element.32) | copy-start | bytes 589828
  29.3 11.3 %collective-permute-start.3 = (f32[16,1,8,256]{3,2,1,0:T(8,128)S(1)}, f32[16,1,8,256]{3,2,1,0:T(8,128)S(1)}, u32[]{:S(2)}, u32[]{:S(2)}) collective-permute-start(f32[16,1,8,256]{3,2,1,0:T(8,128)S(1)} %get-tuple-element.21), channel_id=1, source_target_pairs={{0,4},{4,8},{8,12},{12,16},{16,20},{20,24},{24,28},{28,32},{32,36}... | collective-permute-start | bytes 393224 | tf_op jit(solution)/shard_map/ppermute | solution.py:32
  29.3 11.2 %collective-permute-start.4 = (f32[16,1,8,256]{3,2,1,0:T(8,128)S(1)}, f32[16,1,8,256]{3,2,1,0:T(8,128)S(1)}, u32[]{:S(2)}, u32[]{:S(2)}) collective-permute-start(f32[16,1,8,256]{3,2,1,0:T(8,128)S(1)} %get-tuple-element.20), channel_id=1, source_target_pairs={{4,0},{8,4},{12,8},{16,12},{20,16},{24,20},{28,24},{32,28},{36,32}... | collective-permute-start | bytes 393224 | tf_op jit(solution)/shard_map/ppermute | solution.py:35
  40.6 0.9 copy-start.8
  44.4 10.8 %collective-permute-start.5 = (f32[16,1,8,256]{3,2,1,0:T(8,128)S(1)}, f32[16,1,8,256]{3,2,1,0:T(8,128)S(1)}, u32[]{:S(2)}, u32[]{:S(2)}) collective-permute-start(f32[16,1,8,256]{3,2,1,0:T(8,128)S(1)} %get-tuple-element.18), channel_id=1, source_target_pairs={{0,4},{4,8},{8,12},{12,16},{16,20},{20,24},{24,28},{28,32},{32,36}... | collective-permute-start | bytes 393224 | tf_op jit(solution)/shard_map/ppermute | solution.py:32
  44.5 10.7 %collective-permute-start.6 = (f32[16,1,8,256]{3,2,1,0:T(8,128)S(1)}, f32[16,1,8,256]{3,2,1,0:T(8,128)S(1)}, u32[]{:S(2)}, u32[]{:S(2)}) collective-permute-start(f32[16,1,8,256]{3,2,1,0:T(8,128)S(1)} %get-tuple-element.19), channel_id=1, source_target_pairs={{4,0},{8,4},{12,8},{16,12},{20,16},{24,20},{28,24},{32,28},{36,32}... | collective-permute-start | bytes 393224 | tf_op jit(solution)/shard_map/ppermute | solution.py:35
  57.4 10.8 %collective-permute-start.7 = (f32[16,1,8,256]{3,2,1,0:T(8,128)S(1)}, f32[16,1,8,256]{3,2,1,0:T(8,128)S(1)}, u32[]{:S(2)}, u32[]{:S(2)}) collective-permute-start(f32[16,1,8,256]{3,2,1,0:T(8,128)S(1)} %get-tuple-element.14), channel_id=1, source_target_pairs={{0,4},{4,8},{8,12},{12,16},{16,20},{20,24},{24,28},{28,32},{32,36}... | collective-permute-start | bytes 393224 | tf_op jit(solution)/shard_map/ppermute | solution.py:32
  57.5 10.7 %copy-start.2 = (f32[24,8,256]{2,1,0:T(8,128)S(1)}, f32[24,8,256]{2,1,0:T(8,128)}, u32[]{:S(2)}) copy-start(f32[24,8,256]{2,1,0:T(8,128)} %copy-done.1) | copy-start | bytes 589828
  57.5 10.7 %copy-start.4 = (f32[24,8,256]{2,1,0:T(8,128)S(1)}, f32[24,8,256]{2,1,0:T(8,128)}, u32[]{:S(2)}) copy-start(f32[24,8,256]{2,1,0:T(8,128)} %copy-done.3) | copy-start | bytes 589828
  57.5 10.7 %copy-start.6 = (f32[24,8,256]{2,1,0:T(8,128)S(1)}, f32[24,8,256]{2,1,0:T(8,128)}, u32[]{:S(2)}) copy-start(f32[24,8,256]{2,1,0:T(8,128)} %copy-done.5) | copy-start | bytes 589828
  57.5 10.6 %collective-permute-start.8 = (f32[16,1,8,256]{3,2,1,0:T(8,128)S(1)}, f32[16,1,8,256]{3,2,1,0:T(8,128)S(1)}, u32[]{:S(2)}, u32[]{:S(2)}) collective-permute-start(f32[16,1,8,256]{3,2,1,0:T(8,128)S(1)} %get-tuple-element.15), channel_id=1, source_target_pairs={{4,0},{8,4},{12,8},{16,12},{20,16},{24,20},{28,24},{32,28},{36,32}... | collective-permute-start | bytes 393224 | tf_op jit(solution)/shard_map/ppermute | solution.py:35
  108.3 5.5 %collective-permute-start.9 = (f32[64,64]{0,1:T(8,128)S(1)}, f32[64,64]{0,1:T(8,128)S(1)}, u32[]{:S(2)}, u32[]{:S(2)}) collective-permute-start(f32[64,64]{0,1:T(8,128)S(1)} %fusion.38), channel_id=1, source_target_pairs={{0,4},{4,0},{8,12},{12,8},{16,20},{20,16},{24,28},{28,24},{32,36},... | collective-permute-start | bytes 49160 | tf_op jit(solution)/shard_map/ppermute | solution.py:21
  113.8 3.9 %collective-permute-start.10 = (f32[64,64]{0,1:T(8,128)S(1)}, f32[64,64]{0,1:T(8,128)S(1)}, u32[]{:S(2)}, u32[]{:S(2)}) collective-permute-start(f32[64,64]{0,1:T(8,128)S(1)} %add.96), channel_id=1, source_target_pairs={{0,8},{4,12},{8,0},{12,4},{16,24},{20,28},{24,16},{28,20},{32,40},... | collective-permute-start | bytes 49160 | tf_op jit(solution)/shard_map/ppermute | solution.py:21
  117.8 5.4 %collective-permute-start.11 = (f32[64,64]{0,1:T(8,128)S(1)}, f32[64,64]{0,1:T(8,128)S(1)}, u32[]{:S(2)}, u32[]{:S(2)}) collective-permute-start(f32[64,64]{0,1:T(8,128)S(1)} %add.97), channel_id=1, source_target_pairs={{0,16},{4,20},{8,24},{12,28},{16,0},{20,4},{24,8},{28,12},{32,48},... | collective-permute-start | bytes 49160 | tf_op jit(solution)/shard_map/ppermute | solution.py:21
  123.2 3.9 %collective-permute-start.12 = (f32[64,64]{0,1:T(8,128)S(1)}, f32[64,64]{0,1:T(8,128)S(1)}, u32[]{:S(2)}, u32[]{:S(2)}) collective-permute-start(f32[64,64]{0,1:T(8,128)S(1)} %add.98), channel_id=1, source_target_pairs={{0,32},{4,36},{8,40},{12,44},{16,48},{20,52},{24,56},{28,60},{32,0... | collective-permute-start | bytes 49160 | tf_op jit(solution)/shard_map/ppermute | solution.py:21
  127.1 5.2 %collective-permute-start.13 = (f32[64,64]{0,1:T(8,128)S(1)}, f32[64,64]{0,1:T(8,128)S(1)}, u32[]{:S(2)}, u32[]{:S(2)}) collective-permute-start(f32[64,64]{0,1:T(8,128)S(1)} %add.99), channel_id=1, source_target_pairs={{0,64},{4,68},{8,72},{12,76},{16,80},{20,84},{24,88},{28,92},{32,9... | collective-permute-start | bytes 49160 | tf_op jit(solution)/shard_map/ppermute | solution.py:21
  132.3 7.8 %collective-permute-start.14 = (f32[64,64]{0,1:T(8,128)S(1)}, f32[64,64]{0,1:T(8,128)S(1)}, u32[]{:S(2)}, u32[]{:S(2)}) collective-permute-start(f32[64,64]{0,1:T(8,128)S(1)} %add.100), channel_id=1, source_target_pairs={{0,128},{4,132},{8,136},{12,140},{16,144},{20,148},{24,152},{28,15... | collective-permute-start | bytes 49160 | tf_op jit(solution)/shard_map/ppermute | solution.py:21
